TPU v7x, 512 devices: a whole 4x8x8 slice. The times are simulated.
512 devices in a mesh: head: 8 (over z), blk: 64 (over x, y, core).
Axes of the slice: x: 4, y: 8, z: 8, core: 2. Of those that a mesh axis runs over, the one named last changes fastest.
Arguments:
- vision: bfloat16 [4, 1408, 8192], P(None, 'head', 'blk'), may hold values from -600 to 600
- ln_gain: float32 [1408], P('head'), may hold values from 0.5 to 1.5
- merge_proj: bfloat16 [4, 1408, 1408], P(None, 'head'), may hold values from -0.078125 to 0.078125
- image_slot: int32 [2048], P('blk'), may hold values from 0 to 32764, as said below
- text: bfloat16 [1408, 32768], P('head', 'blk'), may hold values from -600 to 600
- rms_gain: float32 [1408], replicated, may hold values from 0.5 to 1.5
- wqkv: bfloat16 [3, 1408, 1408], P(None, 'head'), may hold values from -0.31835938 to 0.31835938
- pcache: bfloat16 [2, 1408, 131072], P(None, 'head', 'blk'), may hold values from -300 to 300
- block_table: int32 [64, 128], replicated, may hold values from -1 to 4095, as said below
- cache_len: int32 [64], P('blk'), may hold values from 1 to 4096, as said below
Outputs:
- attended: bfloat16 [1408, 32768], P('head', 'blk')
- new_cache: bfloat16 [2, 1408, 32768], P(None, 'head', 'blk')
Inputs may be any that keep to these rules, and one draw needn't show every extreme that they name: `image_slot`: pieces never intersect and start at multiples of 4; the 32 pieces held by one index of blk start in the rows of 32 different requests, and every request receives exactly 32 pieces. `block_table`: row r holds a block number for j < ceil(cache_len[r] / 32) and -1 after; no block number appears twice; index d of blk holds blocks d * 64 to (d+1) * 64 - 1. The longest request has exactly 2 blocks on every index of blk; every other request has at most one block on any index. `cache_len`: exactly one request, the longest, has 4096 cached positions; all others have fewer.
All inputs are finite; a program needn't handle non-finite values.
Results may differ from a plain program's by a relative error of at most 0.025.
The roundings to bfloat16 on the way count: a program that leaves them out, or rounds other values in their place, can miss the bound.
Values may be sent and summed in bfloat16 or wider, within the bound.
A program may use at most 128 MiB of HBM per device.

v0:
```python
import math
import jax
import jax.numpy as jnp
from jax import lax
from jax.sharding import PartitionSpec as P

D = 1408
HD = 88
BS = 32
masked_score = -1e30


def rotary_columns(values, places):
    half = values.shape[1] // 2
    freq_index = jnp.arange(half, dtype=jnp.float32)
    inverse = jnp.exp(freq_index * (-2.0 * math.log(10000.0) / values.shape[1]))
    angles = inverse[:, None] * places[None, :]
    cosine = jnp.cos(angles)[None]
    sine_part = jnp.sin(angles)[None]
    leading = values[:, :half]
    trailing = values[:, half:]
    return jnp.concatenate(
        [leading * cosine - trailing * sine_part, trailing * cosine + leading * sine_part], axis=1
    )


def softmax_part(query_block, keys, values, mask, scale):
    scores = (
        jnp.einsum("hdq,hdk->hqk", query_block, keys, preferred_element_type=jnp.float32) * scale
    )
    scores = jnp.where(mask[None], scores, masked_score)
    highest = jnp.max(scores, axis=2)
    expo = jnp.where(mask[None], jnp.exp(scores - highest[:, :, None]), 0.0)
    total = jnp.sum(expo, axis=2)
    mixed = jnp.einsum("hqk,hdk->hdq", expo, values, precision=lax.Precision.HIGHEST)
    return (mixed, highest, total)


def fold_softmax(first, second):
    mixed_a, high_a, total_a = first
    mixed_b, high_b, total_b = second
    top = jnp.maximum(high_a, high_b)
    factor_a = jnp.exp(high_a - top)
    factor_b = jnp.exp(high_b - top)
    return (
        mixed_a * factor_a[:, None, :] + mixed_b * factor_b[:, None, :],
        top,
        total_a * factor_a + total_b * factor_b,
    )


def unblock(parts):
    mixed, highest, total = parts
    heads_here = mixed.shape[1]
    mixed = jnp.transpose(mixed, (1, 2, 0, 3)).reshape(heads_here, mixed.shape[2], -1)
    highest = jnp.transpose(highest, (1, 0, 2)).reshape(heads_here, -1)
    total = jnp.transpose(total, (1, 0, 2)).reshape(heads_here, -1)
    return (mixed, highest, total)


def shards(
    vision, ln_gain, merge_proj, image_slot, text, rms_gain, wqkv, pcache, block_table, cache_len
):
    local = vision.shape[1]
    groups = vision.shape[2]
    floats = vision.astype(jnp.float32)
    totals, squares = lax.psum((jnp.sum(floats, axis=1), jnp.sum(floats * floats, axis=1)), "head")
    average = totals / D
    spread = squares / D - average * average
    normed_vision = (
        (floats - average[:, None, :])
        * lax.rsqrt(spread + 1e-06)[:, None, :]
        * ln_gain[None, :, None]
    ).astype(jnp.bfloat16)
    partial_rows = jnp.einsum(
        "tcd,tcg->dg", merge_proj, normed_vision, preferred_element_type=jnp.float32
    )
    merged_columns = lax.psum_scatter(partial_rows, "head", scatter_dimension=0, tiled=True).astype(
        jnp.bfloat16
    )
    merged = jnp.transpose(merged_columns)
    devices = lax.axis_size("blk")
    here = lax.axis_index("blk")
    rows_here = text.shape[1]
    pieces = image_slot.shape[0]
    piece_rows = groups // pieces
    lines = jnp.arange(rows_here, dtype=jnp.int32)
    offsets = jnp.arange(piece_rows, dtype=jnp.int32)
    target = image_slot // rows_here
    within = image_slot % rows_here
    select = target[None, :] == jnp.arange(devices, dtype=jnp.int32)[:, None]
    outbound = (
        jnp.dot(
            select.astype(jnp.bfloat16),
            merged.reshape(pieces, piece_rows * local),
            preferred_element_type=jnp.float32,
        )
        .astype(jnp.bfloat16)
        .reshape(devices, piece_rows, local)
    )
    starts = jnp.sum(jnp.where(select, within[None, :] + 1, 0), axis=1) - 1
    arrived, arrived_start = (
        lax.all_to_all(outbound, "blk", split_axis=0, concat_axis=0, tiled=True),
        lax.all_to_all(starts, "blk", split_axis=0, concat_axis=0, tiled=True),
    )
    row_ids = (arrived_start[:, None] + offsets[None, :]).reshape(-1)
    present = jnp.repeat(arrived_start >= 0, piece_rows)
    hits = (row_ids[:, None] == lines[None, :]) & present[:, None]
    placed_rows = jnp.einsum(
        "kl,kr->lr",
        arrived.reshape(devices * piece_rows, local),
        hits.astype(jnp.bfloat16),
        preferred_element_type=jnp.float32,
    ).astype(jnp.bfloat16)
    covered = jnp.any(hits, axis=0)
    placed = jnp.where(covered[None, :], placed_rows, text)
    row_floats = placed.astype(jnp.float32)
    square_sums = lax.psum(jnp.sum(row_floats * row_floats, axis=0), "head")
    gain_here = lax.dynamic_slice_in_dim(rms_gain, lax.axis_index("head") * local, local)
    normed = (row_floats * lax.rsqrt(square_sums / D + 1e-06)[None, :] * gain_here[:, None]).astype(
        jnp.bfloat16
    )
    projected = jnp.einsum(
        "jod,dr->jor",
        wqkv,
        lax.all_gather(normed, "head", axis=0, tiled=True),
        preferred_element_type=jnp.float32,
    )
    heads_here = local // HD
    projected = projected.reshape(3, heads_here, HD, rows_here)
    places = (cache_len[0] + lines).astype(jnp.float32)
    queries = rotary_columns(projected[0], places).astype(jnp.bfloat16)
    new_keys = rotary_columns(projected[1], places).astype(jnp.bfloat16)
    new_values = projected[2].astype(jnp.bfloat16)
    new_cache = jnp.stack(
        [new_keys.reshape(local, rows_here), new_values.reshape(local, rows_here)], axis=0
    )
    block_len = BS
    owned = pcache.shape[2] // block_len
    paged = pcache.reshape(2, local, owned, block_len)
    requests = block_table.shape[0]
    table_width = block_table.shape[1]
    slots_each = table_width // devices
    block_ids = here * owned + jnp.arange(owned, dtype=jnp.int32)
    matches = block_table[None, :, :] == block_ids[:, None, None]
    found = jnp.any(matches, axis=2)
    in_use = jnp.any(found, axis=1)
    owner = jnp.sum(jnp.where(found, jnp.arange(requests, dtype=jnp.int32)[None, :], 0), axis=1)
    logical = jnp.sum(
        jnp.where(matches, jnp.arange(table_width, dtype=jnp.int32)[None, None, :], 0), axis=(1, 2)
    )
    counter = jnp.arange(owned, dtype=jnp.int32)
    earlier = (
        (owner[:, None] == owner[None, :]) & in_use[None, :] & (counter[None, :] < counter[:, None])
    )
    standing = jnp.sum(earlier.astype(jnp.int32), axis=1)
    within_block = jnp.arange(block_len, dtype=jnp.int32)
    block_rows = min(rows_here, 512)
    count_blocks = rows_here // block_rows
    scale = HD ** (-0.5)
    query_blocks = jnp.transpose(
        queries.reshape(heads_here, HD, count_blocks, block_rows), (2, 0, 1, 3)
    )
    first_rows = jnp.arange(count_blocks, dtype=jnp.int32) * block_rows
    destination = owner * slots_each + standing
    routing = (destination[None, :] == jnp.arange(table_width, dtype=jnp.int32)[:, None]) & in_use[
        None, :
    ]
    outgoing = jnp.einsum(
        "wo,cfob->cfwb", routing.astype(jnp.bfloat16), paged, preferred_element_type=jnp.float32
    ).astype(jnp.bfloat16)
    outgoing = outgoing.reshape(2, local, table_width * block_len)
    labels = jnp.sum(jnp.where(routing, logical[None, :] + 1, 0), axis=1) - 1
    labels = labels.reshape(1, 1, table_width)
    blocks_in, labels_in = (
        lax.all_to_all(outgoing, "blk", split_axis=2, concat_axis=2, tiled=True),
        lax.all_to_all(labels, "blk", split_axis=2, concat_axis=2, tiled=True),
    )
    cached_keys = blocks_in[0].reshape(heads_here, HD, -1)
    cached_values = blocks_in[1].reshape(heads_here, HD, -1).astype(jnp.float32)
    label_flat = labels_in.reshape(-1)
    key_places = label_flat[:, None] * block_len + within_block[None, :]
    live = ((label_flat[:, None] >= 0) & (key_places < cache_len[0])).reshape(-1)
    old_mask = jnp.broadcast_to(live[None, :], (block_rows, live.shape[0]))
    new_values_f = new_values.astype(jnp.float32)

    def attend(inputs):
        query_block, first_row = inputs
        causal = (first_row + jnp.arange(block_rows, dtype=jnp.int32))[:, None] >= lines[None, :]
        old_part = softmax_part(query_block, cached_keys, cached_values, old_mask, scale)
        own_part = softmax_part(query_block, new_keys, new_values_f, causal, scale)
        return fold_softmax(old_part, own_part)

    mixed, highest, total = unblock(lax.map(attend, (query_blocks, first_rows)))
    attended = (mixed / total[:, None, :]).astype(jnp.bfloat16).reshape(local, rows_here)
    return (attended, new_cache)


def solution(mesh):
    in_specs = (
        P(None, "head", "blk"),
        P("head"),
        P(None, "head", None),
        P("blk"),
        P("head", "blk"),
        P(),
        P(None, "head", None),
        P(None, "head", "blk"),
        P(),
        P("blk"),
    )
    out_specs = (P("head", "blk"), P(None, "head", "blk"))
    return jax.shard_map(shards, mesh=mesh, in_specs=in_specs, out_specs=out_specs, check_vma=False)
```

profile of v0, /device:TPU:1, one launch (start us, length us, event | category | flops | bytes accessed | tf_op | source)
XLA Modules:
  0.0 288.2 jit_solution(1287686254156349032)
XLA Ops:
  7.2 1.1 convert_reduce_fusion
  8.3 20.3 %all-reduce = (f32[4,128]{1,0:T(4,128)S(1)}, f32[4,128]{1,0:T(4,128)S(1)}) all-reduce(f32[4,128]{1,0:T(4,128)S(1)} %get-tuple-element.23, f32[4,128]{1,0:T(4,128)S(1)} %get-tuple-element.22), channel_id=1, replica_groups=mesh['head'=8,'blk'=64] {'head'}, use_global_device_ids=true, to_apply=%region_11.12 | all-reduce | flops 1024 | bytes 8192 | tf_op jit(solution)/shard_map/psum | solution.py:67
  28.6 1.5 convolution_bitcast_fusion
  30.2 1.1 copy.49
  31.5 0.7 copy.44
  32.2 14.5 %all-to-all-start.2 = ((s32[64,1,1]{2,1,0:T(1,128)}), s32[64,1,1]{2,1,0:T(1,128)S(1)}, u32[]{:S(2)}, u32[]{:S(2)}) async-start(s32[64,1,1]{2,1,0:T(1,128)} %copy.44), calls=%async_computation.2 | async-start | bytes 65536 | tf_op jit(solution)/shard_map/all_to_all | solution.py:104
  46.8 2.4 compare_reduce_fusion
  49.2 0.2 convert_reduce_fusion.1
  49.4 1.4 fusion.8
  50.8 0.1 select_reduce_fusion
  50.9 0.7 copy.43
  51.7 3.7 %copy.38 = bf16[2,176,2048]{1,2,0:T(8,128)(2,1)} copy(bf16[2,176,2048]{2,1,0:T(8,128)(2,1)} %param.17) | data formatting | bytes 2883584 | tf_op args[7]
  55.4 13.9 %reduce-scatter.4.cloned.1.call-done = f32[176,128]{1,0:T(8,128)} async-done(((f32[1408,128]{1,0:T(8,128)}), f32[176,128]{1,0:T(8,128)}) %reduce-scatter.4.cloned.1.call-update) | async-done | bytes 90128
  69.2 1.0 copy.50
  70.2 0.1 reshape.265
  70.4 14.6 %all-to-all-start.1 = ((s32[1,1,128]{1,0,2:T(1,128)}), s32[1,1,128]{1,0,2:T(1,128)S(1)}, u32[]{:S(2)}, u32[]{:S(2)}) async-start(s32[1,1,128]{1,0,2:T(1,128)} %copy.43), calls=%async_computation.1 | async-start | bytes 131072 | tf_op jit(solution)/shard_map/all_to_all | solution.py:177
  85.0 0.3 convolution_convert_fusion.1
  85.3 0.8 reshape.266
  86.1 8.7 %all-to-all-done.1 = s32[1,1,128]{1,0,2:T(1,128)S(1)} async-done(((s32[1,1,128]{1,0,2:T(1,128)}), s32[1,1,128]{1,0,2:T(1,128)S(1)}, u32[]{:S(2)}, u32[]{:S(2)}) %all-to-all-start.1) | async-done | bytes 544 | tf_op jit(solution)/shard_map/all_to_all | solution.py:177
  94.8 4.4 %all-to-all-start.3 = ((bf16[64,4,176]{2,1,0:T(4,128)(2,1)}), bf16[64,4,176]{2,1,0:T(4,128)(2,1)S(1)}, u32[]{:S(2)}, u32[]{:S(2)}) async-start(bf16[64,4,176]{2,1,0:T(4,128)(2,1)} %reshape.266), calls=%async_computation.3 | async-start | bytes 262144 | tf_op jit(solution)/shard_map/all_to_all | solution.py:103
  99.2 4.9 %convert_bitcast_fusion = bf16[2,176,128,32]{2,1,3,0:T(8,128)(2,1)} fusion(bf16[2,176,64,32]{1,3,2,0:T(8,128)(2,1)} %bitcast.47, s32[64]{0:T(128)S(1)} %get-tuple-element.61, pred[64]{0:T(512)(128)(4,1)S(1)} %get-tuple-element.24), kind=kOutput, calls=%fused_computation.13 | convolution fusion | flops 186007552 | bytes 4325696 | tf_op jit(solution)/shard_map/wo,cfob->cfwb/dot_general | solution.py:169
  104.1 7.7 %copy.40 = bf16[2,176,128,32]{1,3,2,0:T(8,128)(2,1)} copy(bf16[2,176,128,32]{2,1,3,0:T(8,128)(2,1)} %convert_bitcast_fusion) | data formatting | bytes 5767168 | tf_op jit(solution)/shard_map/convert_element_type | solution.py:171
  111.8 10.1 %copy.41 = bf16[2,176,4096]{1,0,2:T(2,128)(2,1)} copy(bf16[2,176,4096]{1,2,0:T(8,128)(2,1)} %bitcast.46) | data formatting | bytes 5767168 | tf_op jit(solution)/shard_map/reshape | solution.py:172
  121.9 10.8 %all-to-all-start = ((bf16[2,176,4096]{1,0,2:T(2,128)(2,1)}), bf16[2,176,4096]{1,0,2:T(2,128)(2,1)}, u32[]{:S(2)}, u32[]{:S(2)}) async-start(bf16[2,176,4096]{1,0,2:T(2,128)(2,1)} %copy.41), calls=%async_computation | async-start | bytes 8388608 | tf_op jit(solution)/shard_map/all_to_all | solution.py:176
  132.7 0.8 dynamic_slice.9
  133.5 1.2 reduce.3
  134.8 0.1 and.66
  135.1 0.2 fusion.32
  135.4 0.4 multiply_reduce_fusion
  135.7 13.1 %psum.23 = f32[512]{0:T(512)S(1)} all-reduce(f32[512]{0:T(512)S(1)} %get-tuple-element.55), channel_id=1, replica_groups=mesh['head'=8,'blk'=64] {'head'}, use_global_device_ids=true, to_apply=%region_14.15 | all-reduce | flops 512 | bytes 4096 | tf_op jit(solution)/shard_map/psum | solution.py:118
  148.9 0.8 multiply_convert_fusion
  150.5 0.4 multiply_cosine_fusion
  150.9 2.4 multiply_reduce_fusion.1
  153.2 2.4 compare_reduce_fusion.2
  155.8 34.9 %all-gather.2.cloned.1.call-done = bf16[1408,512]{1,0:T(8,128)(2,1)} async-done(((bf16[176,512]{1,0:T(8,128)(2,1)}), bf16[1408,512]{1,0:T(8,128)(2,1)}) %all-gather.2.cloned.1.call-update) | async-done | bytes 1441808 | tf_op jit(solution)/shard_map/all_gather | solution.py:126
  190.7 2.8 fusion.15
  193.7 0.8 pad_maximum_fusion
  194.6 0.6 fusion.10
  195.3 1.3 copy-done.1
  196.6 0.6 fusion.11
  197.2 31.4 %all-to-all-done = bf16[2,176,4096]{1,0,2:T(2,128)(2,1)} async-done(((bf16[2,176,4096]{1,0,2:T(2,128)(2,1)}), bf16[2,176,4096]{1,0,2:T(2,128)(2,1)}, u32[]{:S(2)}, u32[]{:S(2)}) %all-to-all-start) | async-done | bytes 2883616 | tf_op jit(solution)/shard_map/all_to_all | solution.py:176
  228.6 9.8 %fusion.66 = (bf16[1,176,4096]{1,0,2:T(2,128)(2,1)}, bf16[1,176,4096]{1,0,2:T(2,128)(2,1)}) fusion(bf16[2,176,4096]{1,0,2:T(2,128)(2,1)} %all-to-all-done), kind=kLoop, calls=%fused_computation.118 | loop fusion | bytes 5767168 | tf_op jit(solution)/shard_map/slice | solution.py:180
  238.3 9.6 %copy.42 = bf16[1,176,4096]{2,1,0:T(8,128)(2,1)} copy(bf16[1,176,4096]{1,0,2:T(2,128)(2,1)} %get-tuple-element.41) | data formatting | bytes 2883584 | tf_op jit(solution)/shard_map/slice | solution.py:180
  247.9 9.8 %copy.45 = bf16[1,176,4096]{2,1,0:T(8,128)(2,1)S(1)} copy(bf16[1,176,4096]{1,0,2:T(2,128)(2,1)} %get-tuple-element.42) | data formatting | bytes 2883584 | tf_op jit(solution)/shard_map/slice | solution.py:179
  257.7 3.7 %fusion = (f32[2,512]{1,0:T(2,128)S(1)}, f32[2,512,4096]{2,1,0:T(8,128)S(1)}) fusion(pred[4096]{0:T(1024)(128)(4,1)S(1)} %and.63, bf16[2,88,4096]{2,1,0:T(8,128)(2,1)S(1)} %bitcast.48, bf16[2,44,512]{2,1,0:T(8,128)(2,1)} %copy-done.8, bf16[2,44,512]{2,1,0:T(8,128)(2,1)S(1)} %get-tuple-element.45), kind=kOutput, calls=%fused_computation.2 | convolution fusion | flops 751139840 | bytes 18407424 | tf_op jit(solution)/shard_map/while/body/eval_jaxpr/hdq,hdk->hqk/dot_general | solution.py:29
  261.5 5.1 %fusion.1 = f32[2,512]{1,0:T(2,128)S(1)} fusion(f32[2,512,4096]{2,1,0:T(8,128)S(1)} %get-tuple-element.60, f32[2,512]{1,0:T(2,128)S(1)} %get-tuple-element.59, pred[4096]{0:T(1024)(128)(4,1)S(1)} %and.63), kind=kLoop, calls=%fused_computation.3 | loop fusion | flops 20970496 | bytes 16789504 | tf_op jit(solution)/shard_map/while/body/eval_jaxpr/reduce_sum | solution.py:34
  266.6 1.5 fusion.20
  268.1 13.2 %fusion.29 = bf16[2,88,512]{2,1,0:T(8,128)(2,1)} fusion(f32[2,88,512]{2,1,0:T(8,128)S(1)} %fusion.20, bf16[2,88,4096]{2,1,0:T(8,128)(2,1)S(1)} %bitcast.51, f32[2,512,4096]{2,1,0:T(8,128)S(1)} %get-tuple-element.60, f32[2,512]{1,0:T(2,128)S(1)} %get-tuple-element.59, pred[4096]{0:T(1024)(128)(4,1)S(1)} %and.63, f32[2,512]{1,0:T(2,128)S(1)} %get-tuple-element.28, ...), kind=kOutput, calls=%fused_computation.39 | convolution fusion | flops 4446322688 | bytes 18776064 | tf_op jit(solution)/shard_map/while/body/eval_jaxpr/hqk,hdk->hdq/dot_general | solution.py:35
  (54 shorter events, 1.4 us)
Async XLA Ops:
  7.2 21.5 %copy-start = (bf16[4,176,1408]{2,1,0:T(8,128)(2,1)S(1)}, bf16[4,176,1408]{2,1,0:T(8,128)(2,1)}, u32[]{:S(2)}) copy-start(bf16[4,176,1408]{2,1,0:T(8,128)(2,1)} %param.12) | copy-start | bytes 5947396
  7.2 62.0 %reduce-scatter.4.cloned.1.call-start = ((), (), s32[]{:S(2)}) async-start(), calls=%async_computation.6 | async-start | bytes 811008
  28.6 2.7 copy-start.11
  28.6 18.1 %copy-start.9 = (s32[64,128]{1,0:T(8,128)S(1)}, s32[64,128]{1,0:T(8,128)}, u32[]{:S(2)}) copy-start(s32[64,128]{1,0:T(8,128)} %param.18) | copy-start | bytes 98308
  32.2 38.2 %all-to-all-start.2 = ((s32[64,1,1]{2,1,0:T(1,128)}), s32[64,1,1]{2,1,0:T(1,128)S(1)}, u32[]{:S(2)}, u32[]{:S(2)}) async-start(s32[64,1,1]{2,1,0:T(1,128)} %copy.44), calls=%async_computation.2 | async-start | bytes 65536 | tf_op jit(solution)/shard_map/all_to_all | solution.py:104
  70.4 24.4 %all-to-all-start.1 = ((s32[1,1,128]{1,0,2:T(1,128)}), s32[1,1,128]{1,0,2:T(1,128)S(1)}, u32[]{:S(2)}, u32[]{:S(2)}) async-start(s32[1,1,128]{1,0,2:T(1,128)} %copy.43), calls=%async_computation.1 | async-start | bytes 131072 | tf_op jit(solution)/shard_map/all_to_all | solution.py:177
  94.8 27.1 %all-to-all-start.3 = ((bf16[64,4,176]{2,1,0:T(4,128)(2,1)}), bf16[64,4,176]{2,1,0:T(4,128)(2,1)S(1)}, u32[]{:S(2)}, u32[]{:S(2)}) async-start(bf16[64,4,176]{2,1,0:T(4,128)(2,1)} %reshape.266), calls=%async_computation.3 | async-start | bytes 262144 | tf_op jit(solution)/shard_map/all_to_all | solution.py:103
  121.9 13.5 %copy-start.10 = (bf16[176,512]{1,0:T(8,128)(2,1)S(1)}, bf16[176,512]{1,0:T(8,128)(2,1)}, u32[]{:S(2)}) copy-start(bf16[176,512]{1,0:T(8,128)(2,1)} %param.14) | copy-start | bytes 540676
  121.9 106.7 %all-to-all-start = ((bf16[2,176,4096]{1,0,2:T(2,128)(2,1)}), bf16[2,176,4096]{1,0,2:T(2,128)(2,1)}, u32[]{:S(2)}, u32[]{:S(2)}) async-start(bf16[2,176,4096]{1,0,2:T(2,128)(2,1)} %copy.41), calls=%async_computation | async-start | bytes 8388608 | tf_op jit(solution)/shard_map/all_to_all | solution.py:176
  132.7 58.0 %all-gather.2.cloned.1.call-start = ((), (), s32[]{:S(2)}) async-start(), calls=%async_computation.5 | async-start | bytes 1622016 | tf_op jit(solution)/shard_map/all_gather | solution.py:126
  150.5 44.8 %copy-start.4 = (pred[512,512]{0,1:T(8,128)(4,1)}, pred[512,512]{0,1:T(8,128)(4,1)S(1)}, u32[]{:S(2)}) copy-start(pred[512,512]{0,1:T(8,128)(4,1)S(1)} %iota_compare_fusion) | copy-start | bytes 786436
  193.6 1.0 copy-start.6
  194.6 2.6 copy-start.8
  195.2 1.4 copy-start.1
  261.4 5.2 %copy-start.2 = (f32[2,512,512]{1,2,0:T(8,128)S(1)}, f32[2,512,512]{1,2,0:T(8,128)}, u32[]{:S(2)}) copy-start(f32[2,512,512]{1,2,0:T(8,128)} %copy-done.1) | copy-start | bytes 6291460
  261.5 5.2 %copy-start.5 = (pred[512,512]{0,1:T(8,128)(4,1)S(1)}, pred[512,512]{0,1:T(8,128)(4,1)}, u32[]{:S(2)}) copy-start(pred[512,512]{0,1:T(8,128)(4,1)} %copy-done.4) | copy-start | bytes 786436
  261.5 5.2 %copy-start.7 = (bf16[1,176,512]{2,1,0:T(8,128)(2,1)S(1)}, bf16[1,176,512]{2,1,0:T(8,128)(2,1)}, u32[]{:S(2)}) copy-start(bf16[1,176,512]{2,1,0:T(8,128)(2,1)} %copy-done.6) | copy-start | bytes 540676
  266.6 1.5 copy-start.3
Sparse Core Ops, SparseCore 0:
  31.5 37.7 reduce-scatter.3
  149.8 40.8 all-gather.1
where the time goes:
time: 290 us; the launch traced here: 288 us
  waiting for transfers between devices  88.9 us (31%)
  local copies, waits for them, and re-layouts  57.9 us (20%)
  starting transfers between devices  44.4 us (15%)
  blocking collectives  33.4 us (12%)
  matrix products  28.9 us (10%)
  other arithmetic  19.6 us (7%)
  between operations  15.1 us (5%)
    all_gather x1, waiting for transfers between devices, shards(): lax.all_gather(normed, 'head', axis=0, tiled=True)  34.9 us
    all_to_all x1, waiting for transfers between devices, shards(): lax.all_to_all(outgoing, 'blk', split_axis=2, concat_axis=2, tiled=True)  31.4 us
    psum x1, blocking collectives, shards(): lax.psum((jnp.sum(floats, axis=1), jnp.sum(floats * floats, axis=1)), 'he...  20.3 us
    slice x2, local copies, waits for them, and re-layouts, shards(): cached_values = blocks_in[1].reshape(heads_here, HD, -1).astype(jnp.float32)  19.4 us
    dot_general x2, matrix products, softmax_part(): jnp.einsum('hqk,hdk->hdq', expo, values, precision=lax.Precision.HIGHEST)  14.7 us
    all_to_all x1, starting transfers between devices, shards(): lax.all_to_all(labels, 'blk', split_axis=2, concat_axis=2, tiled=True)  14.6 us
    all_to_all x1, starting transfers between devices, shards(): lax.all_to_all(starts, 'blk', split_axis=0, concat_axis=0, tiled=True)  14.5 us
    unnamed x3, waiting for transfers between devices  13.9 us
  transfers between devices with their start and end apart: 6, of which 4 were waited for; matrix products, arithmetic and copies ran while one was open for 17% of the time, Pallas kernels for 0%

commit v1 on v0

--- a/solution.py
+++ b/solution.py
@@ -115,7 +115,9 @@
     covered = jnp.any(hits, axis=0)
     placed = jnp.where(covered[None, :], placed_rows, text)
     row_floats = placed.astype(jnp.float32)
-    square_sums = lax.psum(jnp.sum(row_floats * row_floats, axis=0), "head")
+    part = jnp.sum(row_floats * row_floats, axis=0)
+    terms = lax.all_gather(part, "head")
+    square_sums = jnp.sum(terms, axis=0)
     gain_here = lax.dynamic_slice_in_dim(rms_gain, lax.axis_index("head") * local, local)
     normed = (row_floats * lax.rsqrt(square_sums / D + 1e-06)[None, :] * gain_here[:, None]).astype(
         jnp.bfloat16

time: 290 us -> 289 us (level)
  waiting for transfers between devices: 88.9 us -> 84 us
  blocking collectives: 33.4 us -> 38.3 us
    all_gather x0 -> x1, blocking collectives: none -> 18 us  [shards(): terms = lax.all_gather(part, 'head')]
    psum x1 -> x0, blocking collectives: 13.1 us -> none  [shards(): square_sums = lax.psum(jnp.sum(row_floats * row_floats, axis=0), 'head')]
    all_to_all x1, waiting for transfers between devices: 31.4 us -> 26.8 us  [shards(): lax.all_to_all(outgoing, 'blk', split_axis=2, concat_axis=2, tiled=True)]
where the time goes in v1:
time: 289 us; the launch traced here: 288 us
  waiting for transfers between devices  84 us (29%)
  local copies, waits for them, and re-layouts  57.9 us (20%)
  starting transfers between devices  44.4 us (15%)
  blocking collectives  38.3 us (13%)
  matrix products  28.9 us (10%)
  other arithmetic  19.4 us (7%)
  between operations  15.1 us (5%)
    all_gather x1, waiting for transfers between devices, shards(): lax.all_gather(normed, 'head', axis=0, tiled=True)  34.5 us
    all_to_all x1, waiting for transfers between devices, shards(): lax.all_to_all(outgoing, 'blk', split_axis=2, concat_axis=2, tiled=True)  26.8 us
    psum x1, blocking collectives, shards(): lax.psum((jnp.sum(floats, axis=1), jnp.sum(floats * floats, axis=1)), 'he...  20.3 us
    slice x2, local copies, waits for them, and re-layouts, shards(): cached_values = blocks_in[1].reshape(heads_here, HD, -1).astype(jnp.float32)  19.4 us
    all_gather x1, blocking collectives, shards(): terms = lax.all_gather(part, 'head')  18 us
    dot_general x2, matrix products, softmax_part(): jnp.einsum('hqk,hdk->hdq', expo, values, precision=lax.Precision.HIGHEST)  14.7 us
    all_to_all x1, starting transfers between devices, shards(): lax.all_to_all(labels, 'blk', split_axis=2, concat_axis=2, tiled=True)  14.6 us
    all_to_all x1, starting transfers between devices, shards(): lax.all_to_all(starts, 'blk', split_axis=0, concat_axis=0, tiled=True)  14.5 us
  transfers between devices with their start and end apart: 6, of which 4 were waited for; matrix products, arithmetic and copies ran while one was open for 17% of the time, Pallas kernels for 0%

profile of v1, /device:TPU:1, one launch (start us, length us, event | category | flops | bytes accessed | tf_op | source)
XLA Modules:
  0.0 287.9 jit_solution(14826711162441645813)
XLA Ops:
  7.2 1.1 convert_reduce_fusion
  8.3 20.3 %all-reduce = (f32[4,128]{1,0:T(4,128)S(1)}, f32[4,128]{1,0:T(4,128)S(1)}) all-reduce(f32[4,128]{1,0:T(4,128)S(1)} %get-tuple-element.23, f32[4,128]{1,0:T(4,128)S(1)} %get-tuple-element.22), channel_id=1, replica_groups=mesh['head'=8,'blk'=64] {'head'}, use_global_device_ids=true, to_apply=%region_11.12 | all-reduce | flops 1024 | bytes 8192 | tf_op jit(solution)/shard_map/psum | solution.py:67
  28.6 1.5 convolution_bitcast_fusion
  30.2 1.1 copy.49
  31.5 0.7 copy.44
  32.2 14.5 %all-to-all-start.2 = ((s32[64,1,1]{2,1,0:T(1,128)}), s32[64,1,1]{2,1,0:T(1,128)S(1)}, u32[]{:S(2)}, u32[]{:S(2)}) async-start(s32[64,1,1]{2,1,0:T(1,128)} %copy.44), calls=%async_computation.2 | async-start | bytes 65536 | tf_op jit(solution)/shard_map/all_to_all | solution.py:104
  46.8 2.4 compare_reduce_fusion
  49.2 0.2 convert_reduce_fusion.1
  49.4 1.4 fusion.8
  50.8 0.1 select_reduce_fusion
  50.9 0.7 copy.43
  51.7 3.7 %copy.38 = bf16[2,176,2048]{1,2,0:T(8,128)(2,1)} copy(bf16[2,176,2048]{2,1,0:T(8,128)(2,1)} %param.17) | data formatting | bytes 2883584 | tf_op args[7]
  55.4 13.9 %reduce-scatter.4.cloned.1.call-done = f32[176,128]{1,0:T(8,128)} async-done(((f32[1408,128]{1,0:T(8,128)}), f32[176,128]{1,0:T(8,128)}) %reduce-scatter.4.cloned.1.call-update) | async-done | bytes 90128
  69.2 1.0 copy.50
  70.2 0.1 reshape.269
  70.4 14.6 %all-to-all-start.1 = ((s32[1,1,128]{1,0,2:T(1,128)}), s32[1,1,128]{1,0,2:T(1,128)S(1)}, u32[]{:S(2)}, u32[]{:S(2)}) async-start(s32[1,1,128]{1,0,2:T(1,128)} %copy.43), calls=%async_computation.1 | async-start | bytes 131072 | tf_op jit(solution)/shard_map/all_to_all | solution.py:179
  85.0 0.3 convolution_convert_fusion.1
  85.3 0.8 reshape.270
  86.1 8.7 %all-to-all-done.1 = s32[1,1,128]{1,0,2:T(1,128)S(1)} async-done(((s32[1,1,128]{1,0,2:T(1,128)}), s32[1,1,128]{1,0,2:T(1,128)S(1)}, u32[]{:S(2)}, u32[]{:S(2)}) %all-to-all-start.1) | async-done | bytes 544 | tf_op jit(solution)/shard_map/all_to_all | solution.py:179
  94.8 4.4 %all-to-all-start.3 = ((bf16[64,4,176]{2,1,0:T(4,128)(2,1)}), bf16[64,4,176]{2,1,0:T(4,128)(2,1)S(1)}, u32[]{:S(2)}, u32[]{:S(2)}) async-start(bf16[64,4,176]{2,1,0:T(4,128)(2,1)} %reshape.270), calls=%async_computation.3 | async-start | bytes 262144 | tf_op jit(solution)/shard_map/all_to_all | solution.py:103
  99.2 4.9 %convert_bitcast_fusion = bf16[2,176,128,32]{2,1,3,0:T(8,128)(2,1)} fusion(bf16[2,176,64,32]{1,3,2,0:T(8,128)(2,1)} %bitcast.48, s32[64]{0:T(128)S(1)} %get-tuple-element.61, pred[64]{0:T(512)(128)(4,1)S(1)} %get-tuple-element.24), kind=kOutput, calls=%fused_computation.13 | convolution fusion | flops 186007552 | bytes 4325696 | tf_op jit(solution)/shard_map/wo,cfob->cfwb/dot_general | solution.py:171
  104.1 7.7 %copy.40 = bf16[2,176,128,32]{1,3,2,0:T(8,128)(2,1)} copy(bf16[2,176,128,32]{2,1,3,0:T(8,128)(2,1)} %convert_bitcast_fusion) | data formatting | bytes 5767168 | tf_op jit(solution)/shard_map/convert_element_type | solution.py:173
  111.8 10.1 %copy.41 = bf16[2,176,4096]{1,0,2:T(2,128)(2,1)} copy(bf16[2,176,4096]{1,2,0:T(8,128)(2,1)} %bitcast.47) | data formatting | bytes 5767168 | tf_op jit(solution)/shard_map/reshape | solution.py:174
  121.9 10.8 %all-to-all-start = ((bf16[2,176,4096]{1,0,2:T(2,128)(2,1)}), bf16[2,176,4096]{1,0,2:T(2,128)(2,1)}, u32[]{:S(2)}, u32[]{:S(2)}) async-start(bf16[2,176,4096]{1,0,2:T(2,128)(2,1)} %copy.41), calls=%async_computation | async-start | bytes 8388608 | tf_op jit(solution)/shard_map/all_to_all | solution.py:178
  132.7 0.8 dynamic_slice.9
  133.5 1.2 reduce.4
  134.8 0.1 and.66
  135.1 0.2 fusion.32
  135.4 0.4 multiply_reduce_fusion
  135.7 18.0 %all-gather.1 = f32[8,1,512]{2,1,0:T(1,128)S(1)} all-gather(f32[1,1,512]{2,1,0:T(1,128)S(1)} %bitcast.56), channel_id=2, replica_groups=mesh['head'=8,'blk'=64] {'head'}, dimensions={0}, use_global_device_ids=true | all-gather | bytes 18432 | tf_op jit(solution)/shard_map/all_gather | solution.py:119
  153.8 0.8 multiply_convert_fusion
  155.4 0.4 multiply_cosine_fusion
  155.8 2.4 multiply_reduce_fusion.1
  158.1 2.4 compare_reduce_fusion.2
  160.7 34.5 %all-gather.4.cloned.1.call-done = bf16[1408,512]{1,0:T(8,128)(2,1)} async-done(((bf16[176,512]{1,0:T(8,128)(2,1)}), bf16[1408,512]{1,0:T(8,128)(2,1)}) %all-gather.4.cloned.1.call-update) | async-done | bytes 1441808 | tf_op jit(solution)/shard_map/all_gather | solution.py:128
  195.3 2.8 fusion.15
  198.3 0.8 pad_maximum_fusion
  199.2 0.6 fusion.10
  199.8 1.3 copy-done.1
  201.1 0.6 fusion.11
  201.7 26.8 %all-to-all-done = bf16[2,176,4096]{1,0,2:T(2,128)(2,1)} async-done(((bf16[2,176,4096]{1,0,2:T(2,128)(2,1)}), bf16[2,176,4096]{1,0,2:T(2,128)(2,1)}, u32[]{:S(2)}, u32[]{:S(2)}) %all-to-all-start) | async-done | bytes 2883616 | tf_op jit(solution)/shard_map/all_to_all | solution.py:178
  228.6 9.8 %fusion.66 = (bf16[1,176,4096]{1,0,2:T(2,128)(2,1)}, bf16[1,176,4096]{1,0,2:T(2,128)(2,1)}) fusion(bf16[2,176,4096]{1,0,2:T(2,128)(2,1)} %all-to-all-done), kind=kLoop, calls=%fused_computation.118 | loop fusion | bytes 5767168 | tf_op jit(solution)/shard_map/slice | solution.py:182
  238.3 9.6 %copy.42 = bf16[1,176,4096]{2,1,0:T(8,128)(2,1)} copy(bf16[1,176,4096]{1,0,2:T(2,128)(2,1)} %get-tuple-element.41) | data formatting | bytes 2883584 | tf_op jit(solution)/shard_map/slice | solution.py:182
  247.9 9.8 %copy.45 = bf16[1,176,4096]{2,1,0:T(8,128)(2,1)S(1)} copy(bf16[1,176,4096]{1,0,2:T(2,128)(2,1)} %get-tuple-element.42) | data formatting | bytes 2883584 | tf_op jit(solution)/shard_map/slice | solution.py:181
  257.7 3.7 %fusion = (f32[2,512]{1,0:T(2,128)S(1)}, f32[2,512,4096]{2,1,0:T(8,128)S(1)}) fusion(pred[4096]{0:T(1024)(128)(4,1)S(1)} %and.63, bf16[2,88,4096]{2,1,0:T(8,128)(2,1)S(1)} %bitcast.49, bf16[2,44,512]{2,1,0:T(8,128)(2,1)} %copy-done.8, bf16[2,44,512]{2,1,0:T(8,128)(2,1)S(1)} %get-tuple-element.45), kind=kOutput, calls=%fused_computation.2 | convolution fusion | flops 751139840 | bytes 18407424 | tf_op jit(solution)/shard_map/while/body/eval_jaxpr/hdq,hdk->hqk/dot_general | solution.py:29
  261.5 4.9 %fusion.1 = f32[2,512]{1,0:T(2,128)S(1)} fusion(f32[2,512,4096]{2,1,0:T(8,128)S(1)} %get-tuple-element.60, f32[2,512]{1,0:T(2,128)S(1)} %get-tuple-element.59, pred[4096]{0:T(1024)(128)(4,1)S(1)} %and.63), kind=kLoop, calls=%fused_computation.3 | loop fusion | flops 20970496 | bytes 16789504 | tf_op jit(solution)/shard_map/while/body/eval_jaxpr/reduce_sum | solution.py:34
  266.4 1.5 fusion.20
  267.9 13.2 %fusion.29 = bf16[2,88,512]{2,1,0:T(8,128)(2,1)} fusion(f32[2,88,512]{2,1,0:T(8,128)S(1)} %fusion.20, bf16[2,88,4096]{2,1,0:T(8,128)(2,1)S(1)} %bitcast.52, f32[2,512,4096]{2,1,0:T(8,128)S(1)} %get-tuple-element.60, f32[2,512]{1,0:T(2,128)S(1)} %get-tuple-element.59, pred[4096]{0:T(1024)(128)(4,1)S(1)} %and.63, f32[2,512]{1,0:T(2,128)S(1)} %get-tuple-element.28, ...), kind=kOutput, calls=%fused_computation.39 | convolution fusion | flops 4446322688 | bytes 18776064 | tf_op jit(solution)/shard_map/while/body/eval_jaxpr/hqk,hdk->hdq/dot_general | solution.py:35
  (55 shorter events, 1.4 us)
Async XLA Ops:
  7.2 21.5 %copy-start = (bf16[4,176,1408]{2,1,0:T(8,128)(2,1)S(1)}, bf16[4,176,1408]{2,1,0:T(8,128)(2,1)}, u32[]{:S(2)}) copy-start(bf16[4,176,1408]{2,1,0:T(8,128)(2,1)} %param.12) | copy-start | bytes 5947396
  7.2 62.0 %reduce-scatter.4.cloned.1.call-start = ((), (), s32[]{:S(2)}) async-start(), calls=%async_computation.6 | async-start | bytes 811008
  28.6 2.7 copy-start.11
  28.6 18.1 %copy-start.9 = (s32[64,128]{1,0:T(8,128)S(1)}, s32[64,128]{1,0:T(8,128)}, u32[]{:S(2)}) copy-start(s32[64,128]{1,0:T(8,128)} %param.18) | copy-start | bytes 98308
  32.2 38.2 %all-to-all-start.2 = ((s32[64,1,1]{2,1,0:T(1,128)}), s32[64,1,1]{2,1,0:T(1,128)S(1)}, u32[]{:S(2)}, u32[]{:S(2)}) async-start(s32[64,1,1]{2,1,0:T(1,128)} %copy.44), calls=%async_computation.2 | async-start | bytes 65536 | tf_op jit(solution)/shard_map/all_to_all | solution.py:104
  70.4 24.4 %all-to-all-start.1 = ((s32[1,1,128]{1,0,2:T(1,128)}), s32[1,1,128]{1,0,2:T(1,128)S(1)}, u32[]{:S(2)}, u32[]{:S(2)}) async-start(s32[1,1,128]{1,0,2:T(1,128)} %copy.43), calls=%async_computation.1 | async-start | bytes 131072 | tf_op jit(solution)/shard_map/all_to_all | solution.py:179
  94.8 27.1 %all-to-all-start.3 = ((bf16[64,4,176]{2,1,0:T(4,128)(2,1)}), bf16[64,4,176]{2,1,0:T(4,128)(2,1)S(1)}, u32[]{:S(2)}, u32[]{:S(2)}) async-start(bf16[64,4,176]{2,1,0:T(4,128)(2,1)} %reshape.270), calls=%async_computation.3 | async-start | bytes 262144 | tf_op jit(solution)/shard_map/all_to_all | solution.py:103
  121.9 13.5 %copy-start.10 = (bf16[176,512]{1,0:T(8,128)(2,1)S(1)}, bf16[176,512]{1,0:T(8,128)(2,1)}, u32[]{:S(2)}) copy-start(bf16[176,512]{1,0:T(8,128)(2,1)} %param.14) | copy-start | bytes 540676
  121.9 106.7 %all-to-all-start = ((bf16[2,176,4096]{1,0,2:T(2,128)(2,1)}), bf16[2,176,4096]{1,0,2:T(2,128)(2,1)}, u32[]{:S(2)}, u32[]{:S(2)}) async-start(bf16[2,176,4096]{1,0,2:T(2,128)(2,1)} %copy.41), calls=%async_computation | async-start | bytes 8388608 | tf_op jit(solution)/shard_map/all_to_all | solution.py:178
  132.7 62.6 %all-gather.4.cloned.1.call-start = ((), (), s32[]{:S(2)}) async-start(), calls=%async_computation.5 | async-start | bytes 1622016 | tf_op jit(solution)/shard_map/all_gather | solution.py:128
  155.3 44.4 %copy-start.4 = (pred[512,512]{0,1:T(8,128)(4,1)}, pred[512,512]{0,1:T(8,128)(4,1)S(1)}, u32[]{:S(2)}) copy-start(pred[512,512]{0,1:T(8,128)(4,1)S(1)} %iota_compare_fusion) | copy-start | bytes 786436
  198.1 1.0 copy-start.6
  199.1 2.6 copy-start.8
  199.8 1.4 copy-start.1
  261.4 4.9 %copy-start.2 = (f32[2,512,512]{1,2,0:T(8,128)S(1)}, f32[2,512,512]{1,2,0:T(8,128)}, u32[]{:S(2)}) copy-start(f32[2,512,512]{1,2,0:T(8,128)} %copy-done.1) | copy-start | bytes 6291460
  261.5 4.9 %copy-start.5 = (pred[512,512]{0,1:T(8,128)(4,1)S(1)}, pred[512,512]{0,1:T(8,128)(4,1)}, u32[]{:S(2)}) copy-start(pred[512,512]{0,1:T(8,128)(4,1)} %copy-done.4) | copy-start | bytes 786436
  261.5 4.9 %copy-start.7 = (bf16[1,176,512]{2,1,0:T(8,128)(2,1)S(1)}, bf16[1,176,512]{2,1,0:T(8,128)(2,1)}, u32[]{:S(2)}) copy-start(bf16[1,176,512]{2,1,0:T(8,128)(2,1)} %copy-done.6) | copy-start | bytes 540676
  266.4 1.5 copy-start.3
Sparse Core Ops, SparseCore 0:
  31.5 37.7 reduce-scatter.3
  154.7 40.4 all-gather.3
